TPU v7x, 512 devices: a whole 4x8x8 slice. The times are simulated.
512 devices in a mesh: rep: 64 (over x, z_hi, y), ctx: 8 (over z_lo, core).
Axes of the slice: x: 4, y: 8, z: 8 (z_hi: 2, z_lo: 4; z = z_hi * 4 + z_lo), core: 2. Of those that a mesh axis runs over, the one named last changes fastest.
Arguments:
- activations: bfloat16 [64, 1024, 4096], P('rep', 'ctx'), may hold values from -6 to 6
- queries: bfloat16 [64, 1024, 2048], P('rep', 'ctx'), may hold values from -110 to 110
- key_states: bfloat16 [64, 1024, 512], P('rep', 'ctx'), may hold values from -4 to 4
- targets: bfloat16 [64, 1024, 2048], P('rep', 'ctx'), may hold values from -1.5 to 1.5
- value_weight: bfloat16 [64, 4096, 512], P('rep', 'ctx'), may hold values from -5 to 5
- tracker: bfloat16 [64, 4096, 512], P('rep', 'ctx'), may hold values from -5 to 5
- old_gradient: bfloat16 [64, 4096, 512], P('rep', 'ctx'), may hold values from -5 to 5
Outputs:
- new_weight: bfloat16 [64, 4096, 512], P('rep', 'ctx')
- new_tracker: bfloat16 [64, 4096, 512], P('rep', 'ctx')
All inputs are finite; a program needn't handle non-finite values.
Results may differ from a plain program's by a relative error of at most 0.0095.
Values may be sent and summed in bfloat16 or wider, within the bound.
A program may use at most 64 MiB of HBM per device.

v0:
```python
import jax
import jax.numpy as jnp
from jax import lax
from jax.sharding import PartitionSpec as P

HEADS = 16
KV_HEADS = 4
HEAD_DIM = 128
ROUND = 3
step_size = 0.25
loss_weight = 16.0


def partner(shard, axis, apart):
    return lax.ppermute(shard, axis, [(i, i ^ 1 << apart) for i in range(lax.axis_size(axis))])


def local(activations, queries, key_states, targets, value_weight, tracker, old_gradient):
    token_block = activations[0]
    tokens_here = token_block.shape[0]
    value_scale = token_block.shape[1] ** (-0.5)
    grouping = HEADS // KV_HEADS
    own_weight = value_weight[0]
    weight_full = own_weight.astype(jnp.float32)
    track_full = tracker[0].astype(jnp.float32)
    old_full = old_gradient[0].astype(jnp.float32)
    feature_cols = lax.all_to_all(token_block, "ctx", split_axis=1, concat_axis=0, tiled=True)
    local_values = (
        jnp.dot(
            token_block,
            lax.all_gather(own_weight, "ctx", axis=0, tiled=True),
            preferred_element_type=jnp.float32,
        )
        * value_scale
    ).astype(jnp.bfloat16)
    all_keys, all_values = (
        lax.all_gather(key_states[0], "ctx", axis=0, tiled=True),
        lax.all_gather(local_values, "ctx", axis=0, tiled=True),
    )
    seq_total = all_keys.shape[0]
    query_heads = queries[0].reshape(tokens_here, KV_HEADS, grouping, HEAD_DIM)
    key_heads = all_keys.reshape(seq_total, KV_HEADS, HEAD_DIM)
    value_heads = all_values.reshape(seq_total, KV_HEADS, HEAD_DIM)
    scores = jnp.einsum(
        "ikgd,jkd->kgij", query_heads, key_heads, preferred_element_type=jnp.float32
    ) * HEAD_DIM ** (-0.5)
    query_pos = lax.axis_index("ctx") * tokens_here + jnp.arange(tokens_here)
    key_pos = jnp.arange(seq_total)
    allowed = key_pos[None, :] <= query_pos[:, None]
    scores = jnp.where(allowed, scores, -jnp.inf)
    highest = jnp.max(scores, axis=-1, keepdims=True)
    raised = jnp.exp(scores - highest)
    probabilities = (raised / jnp.sum(raised, axis=-1, keepdims=True)).astype(jnp.bfloat16)
    attended = jnp.einsum(
        "kgij,jkd->ikgd", probabilities, value_heads, preferred_element_type=jnp.float32
    )
    attended = attended.reshape(tokens_here, HEADS * HEAD_DIM)
    out_cot = (loss_weight * (attended - targets[0].astype(jnp.float32))).astype(jnp.bfloat16)
    cot_heads = out_cot.reshape(tokens_here, KV_HEADS, grouping, HEAD_DIM)
    value_terms = jnp.einsum(
        "kgij,ikgd->jkd", probabilities, cot_heads, preferred_element_type=jnp.float32
    )
    value_terms = value_terms.reshape(seq_total, KV_HEADS * HEAD_DIM)
    value_cot16 = lax.psum(value_terms, "ctx").astype(jnp.bfloat16)
    gradient = (
        jnp.einsum("tc,tv->cv", feature_cols, value_cot16, preferred_element_type=jnp.float32)
        * value_scale
    )
    track_half = track_full + gradient - old_full
    moved = weight_full - step_size * track_half
    peer_both = partner(jnp.stack((moved, track_half)), "rep", ROUND)
    new_weight = ((moved + peer_both[0]) * 0.5).astype(jnp.bfloat16)
    new_tracker = ((track_half + peer_both[1]) * 0.5).astype(jnp.bfloat16)
    return (new_weight[None], new_tracker[None])


def solution(mesh):
    return jax.shard_map(
        local,
        mesh=mesh,
        in_specs=(
            P("rep", "ctx", None),
            P("rep", "ctx", None),
            P("rep", "ctx", None),
            P("rep", "ctx", None),
            P("rep", "ctx", None),
            P("rep", "ctx", None),
            P("rep", "ctx", None),
        ),
        out_specs=(P("rep", "ctx", None), P("rep", "ctx", None)),
        check_vma=False,
    )
```

profile of v0, /device:TPU:1, one launch (start us, length us, event | category | flops | bytes accessed | tf_op | source)
XLA Modules:
  0.0 347.0 jit_solution(10551125804644642913)
XLA Ops:
  7.2 0.0 copy-start
  7.2 0.0 copy-start.2
  7.2 0.0 copy-start.1
  7.2 0.0 all-gather.8.cloned.1.call-start
  7.2 0.7 all-gather.8.cloned.1.call-update
  7.9 0.0 all-gather.10.cloned.1.call-start
  8.0 1.7 copy.29
  9.7 0.0 all-gather.10.cloned.1.call-update
  9.7 2.3 copy.36
  11.9 10.3 %all-to-all-start = ((bf16[128,8,512]{0,2,1:T(8,128)(2,1)}), bf16[128,8,512]{0,2,1:T(8,128)(2,1)S(1)}, u32[]{:S(2)}, u32[]{:S(2)}) async-start(bf16[128,8,512]{0,2,1:T(8,128)(2,1)} %bitcast.16), calls=%async_computation | async-start | bytes 2097152 | tf_op jit(solution)/shard_map/all_to_all | solution.py:27
  22.2 0.0 all-gather.6.cloned.1.call-start
  22.2 64.3 %all-gather.8.cloned.1.call-done = bf16[1,4096,512]{2,1,0:T(8,128)(2,1)} async-done(((bf16[1,512,512]{2,1,0:T(8,128)(2,1)}), bf16[1,4096,512]{2,1,0:T(8,128)(2,1)}) %all-gather.8.cloned.1.call-update) | async-done | bytes 4194320 | tf_op jit(solution)/shard_map/all_gather | solution.py:31
  86.6 3.9 %fusion.19 = bf16[128,512]{1,0:T(8,128)(2,1)} fusion(bf16[1,4096,512]{2,1,0:T(8,128)(2,1)} %all-gather.8.cloned.1.call-done, bf16[1,128,4096]{2,1,0:T(8,128)(2,1)} %param.7), kind=kOutput, calls=%fused_computation.22 | convolution fusion | flops 537001984 | bytes 5373952 | tf_op jit(solution)/shard_map/dot_general | solution.py:29
  90.4 0.0 all-gather.6.cloned.1.call-update
  90.5 0.0 copy-done
  90.5 0.2 copy.27
  90.7 0.0 copy-done.2
  90.7 1.2 reshape_squeeze.3
  91.9 0.0 copy-done.1
  91.9 1.2 copy.34
  93.1 1.3 copy.28
  94.3 2.0 copy.38
  96.4 0.1 iota_compare_fusion
  96.5 0.0 all-to-all-done
  96.5 1.4 copy.37
  97.8 27.6 %all-gather.10.cloned.1.call-done = bf16[1,1024,512]{1,2,0:T(8,128)(2,1)} async-done(((bf16[1,128,512]{1,2,0:T(8,128)(2,1)}), bf16[1,1024,512]{1,2,0:T(8,128)(2,1)}) %all-gather.10.cloned.1.call-update) | async-done | bytes 1048592 | tf_op jit(solution)/shard_map/all_gather | solution.py:37
  125.4 7.3 %fusion.44 = (f32[4,4,128]{2,1,0:T(4,128)S(1)}, f32[4,4,128,1024]{2,3,1,0:T(8,128)}) fusion(pred[128,1024]{0,1:T(8,128)(4,1)S(1)} %iota_compare_fusion, bf16[1024,4,128,1]{0,2,3,1:T(8,128)(2,1)} %bitcast.105, bf16[128,4,4,128]{3,2,1,0:T(4,128)(2,1)} %reshape_squeeze.3), kind=kOutput, calls=%fused_computation.46 | convolution fusion | flops 545260544 | bytes 10100736 | tf_op jit(solution)/shard_map/sub | solution.py:52
  132.7 31.0 %all-gather.6.cloned.1.call-done = bf16[1024,512]{1,0:T(8,128)(2,1)} async-done(((bf16[128,512]{1,0:T(8,128)(2,1)}), bf16[1024,512]{1,0:T(8,128)(2,1)}) %all-gather.6.cloned.1.call-update) | async-done | bytes 1048592 | tf_op jit(solution)/shard_map/all_gather | solution.py:38
  163.6 2.3 copy.46
  165.9 8.5 %fusion.15 = f32[4,128,1024,1]{2,1,3,0:T(8,128)S(1)} fusion(f32[128,4,4,128]{0,3,2,1:T(8,128)} %bitcast.102, bf16[1024,4,128,1]{0,2,3,1:T(8,128)(2,1)} %bitcast.104, f32[4,4,128,1024]{2,3,1,0:T(8,128)} %get-tuple-element.11, f32[4,4,128]{2,1,0:T(4,128)S(1)} %get-tuple-element.10), kind=kOutput, calls=%fused_computation.20 | convolution fusion | flops 1082916864 | bytes 12591104 | tf_op jit(solution)/shard_map/kgij,ikgd->jkd/dot_general | solution.py:60
  174.4 62.7 %all-reduce.1 = bf16[1024,512]{0,1:T(8,128)(2,1)} all-reduce(f32[1024,512]{0,1:T(8,128)S(1)} %bitcast.101), channel_id=1, replica_groups=mesh['rep'=64,'ctx'=8] {'ctx'}, use_global_device_ids=true, to_apply=%region_2.3 | all-reduce | flops 524288 | bytes 3145728 | tf_op jit(solution)/shard_map/psum | solution.py:64
  237.1 2.4 fusion.13
  239.5 0.2 fusion.30
  239.7 0.2 pad_maximum_fusion
  239.9 6.0 %collective-permute-start = (f32[2,512,512]{1,2,0:T(8,128)S(1)}, f32[2,512,512]{1,2,0:T(8,128)S(1)}, u32[]{:S(2)}, u32[]{:S(2)}) collective-permute-start(f32[2,512,512]{1,2,0:T(8,128)S(1)} %pad_maximum_fusion), channel_id=1, source_target_pairs={{0,64},{8,72},{16,80},{24,88},{32,96},{40,104},{48,112},{56,120},{... | collective-permute-start | bytes 6291464 | tf_op jit(solution)/shard_map/ppermute | solution.py:15
  245.9 92.1 %collective-permute-done = f32[2,512,512]{1,2,0:T(8,128)S(1)} collective-permute-done((f32[2,512,512]{1,2,0:T(8,128)S(1)}, f32[2,512,512]{1,2,0:T(8,128)S(1)}, u32[]{:S(2)}, u32[]{:S(2)}) %collective-permute-start) | collective-permute-done | bytes 2097184 | tf_op jit(solution)/shard_map/ppermute | solution.py:15
  338.0 0.5 fusion.32
  338.5 1.0 copy.39
  339.5 1.0 copy.40
  (1 shorter events, 0.0 us)
Async XLA Ops:
  7.2 83.3 %copy-start = (bf16[1,512,512]{2,1,0:T(8,128)(2,1)S(1)}, bf16[1,512,512]{2,1,0:T(8,128)(2,1)}, u32[]{:S(2)}) copy-start(bf16[1,512,512]{2,1,0:T(8,128)(2,1)} %param.11) | copy-start | bytes 1572868
  7.2 83.5 %copy-start.2 = (bf16[1,128,2048]{2,1,0:T(8,128)(2,1)S(1)}, bf16[1,128,2048]{2,1,0:T(8,128)(2,1)}, u32[]{:S(2)}) copy-start(bf16[1,128,2048]{2,1,0:T(8,128)(2,1)} %param.8) | copy-start | bytes 1572868
  7.2 84.7 %copy-start.1 = (bf16[1,128,2048]{2,1,0:T(8,128)(2,1)S(1)}, bf16[1,128,2048]{2,1,0:T(8,128)(2,1)}, u32[]{:S(2)}) copy-start(bf16[1,128,2048]{2,1,0:T(8,128)(2,1)} %param.10) | copy-start | bytes 1572868
  7.2 79.4 %all-gather.8.cloned.1.call-start = ((), (), s32[]{:S(2)}) async-start(), calls=%async_computation.2 | async-start | bytes 4718592 | tf_op jit(solution)/shard_map/all_gather | solution.py:31
  7.9 117.5 %all-gather.10.cloned.1.call-start = ((), (), s32[]{:S(2)}) async-start(), calls=%async_computation.3 | async-start | bytes 1179648 | tf_op jit(solution)/shard_map/all_gather | solution.py:37
  11.9 84.5 %all-to-all-start = ((bf16[128,8,512]{0,2,1:T(8,128)(2,1)}), bf16[128,8,512]{0,2,1:T(8,128)(2,1)S(1)}, u32[]{:S(2)}, u32[]{:S(2)}) async-start(bf16[128,8,512]{0,2,1:T(8,128)(2,1)} %bitcast.16), calls=%async_computation | async-start | bytes 2097152 | tf_op jit(solution)/shard_map/all_to_all | solution.py:27
  22.2 141.4 %all-gather.6.cloned.1.call-start = ((), (), s32[]{:S(2)}) async-start(), calls=%async_computation.1 | async-start | bytes 1179648 | tf_op jit(solution)/shard_map/all_gather | solution.py:38
  239.9 98.1 %collective-permute-start = (f32[2,512,512]{1,2,0:T(8,128)S(1)}, f32[2,512,512]{1,2,0:T(8,128)S(1)}, u32[]{:S(2)}, u32[]{:S(2)}) collective-permute-start(f32[2,512,512]{1,2,0:T(8,128)S(1)} %pad_maximum_fusion), channel_id=1, source_target_pairs={{0,64},{8,72},{16,80},{24,88},{32,96},{40,104},{48,112},{56,120},{... | collective-permute-start | bytes 6291464 | tf_op jit(solution)/shard_map/ppermute | solution.py:15
Sparse Core Ops, SparseCore 0:
  10.1 76.4 all-gather.7
  88.6 36.7 all-gather.9
  127.5 36.1 all-gather.5
where the time goes:
time: 347 us
  waiting for transfers between devices  216 us (62%)
  blocking collectives  62.7 us (18%)
  matrix products  22 us (6%)
  starting transfers between devices  16.4 us (5%)
  local copies, waits for them, and re-layouts  15.5 us (4%)
  between operations  13.8 us (4%)
    ppermute x1, waiting for transfers between devices, partner(): lax.ppermute(shard, axis, [(i, i ^ 1 << apart) for i in range(lax.axis_si...  92.1 us
    all_gather x1, waiting for transfers between devices, local(): lax.all_gather(own_weight, 'ctx', axis=0, tiled=True)  64.3 us
    psum x1, blocking collectives, local(): value_cot16 = lax.psum(value_terms, 'ctx').astype(jnp.bfloat16)  62.7 us
    all_gather x1, waiting for transfers between devices, local(): lax.all_gather(local_values, 'ctx', axis=0, tiled=True)  31 us
    all_gather x1, waiting for transfers between devices, local(): lax.all_gather(key_states[0], 'ctx', axis=0, tiled=True)  27.6 us
    all_to_all x1, starting transfers between devices, local(): lax.all_to_all(token_block, 'ctx', split_axis=1, concat_axis=0, tiled=True)  10.3 us
    unnamed x13, local copies, waits for them, and re-layouts  9.48 us
    dot_general x1, matrix products, local(): jnp.einsum('kgij,ikgd->jkd', probabilities, cot_heads, preferred_element_...  8.46 us
  transfers between devices with their start and end apart: 5, of which 4 were waited for; matrix products, arithmetic and copies ran while one was open for 6% of the time, Pallas kernels for 0%

commit v1 on v0

--- a/solution.py
+++ b/solution.py
@@ -34,7 +34,9 @@
         * value_scale
     ).astype(jnp.bfloat16)
     all_keys, all_values = (
-        lax.all_gather(key_states[0], "ctx", axis=0, tiled=True),
+        jnp.concatenate(
+            lax.all_to_all(jnp.stack([key_states[0]] * lax.axis_size("ctx")), "ctx", 0, 0), axis=0
+        ),
         lax.all_gather(local_values, "ctx", axis=0, tiled=True),
     )
     seq_total = all_keys.shape[0]

time: 347 us -> 334 us (0.963)
  waiting for transfers between devices: 216 us -> 190 us
  starting transfers between devices: 16.4 us -> 22.8 us
  local copies, waits for them, and re-layouts: 15.5 us -> 21.1 us
    all_to_all x0 -> x1, waiting for transfers between devices: none -> 33.3 us  [local(): lax.all_to_all(jnp.stack([key_states[0]] * lax.axis_size('ctx')), 'ctx',...]
    all_gather x1 -> x0, waiting for transfers between devices: 27.6 us -> none  [local(): lax.all_gather(key_states[0], 'ctx', axis=0, tiled=True)]
    all_gather x1, waiting for transfers between devices: 64.3 us -> 44.6 us  [local(): lax.all_gather(own_weight, 'ctx', axis=0, tiled=True)]
    all_gather x1, waiting for transfers between devices: 31 us -> 19.1 us  [local(): lax.all_gather(local_values, 'ctx', axis=0, tiled=True)]
    all_to_all x0 -> x1, starting transfers between devices: none -> 10.3 us  [local(): lax.all_to_all(jnp.stack([key_states[0]] * lax.axis_size('ctx')), 'ctx',...]
    all_to_all x1, starting transfers between devices: 10.3 us -> 6.5 us  [local(): lax.all_to_all(token_block, 'ctx', split_axis=1, concat_axis=0, tiled=True)]
    another operation x0 -> x3, local copies, waits for them, and re-layouts: none -> 3.65 us  [the longest x1 1.51 us: local(): key_heads = all_keys.reshape(seq_total, KV_HEADS, HEAD_DIM)]
    unnamed x13 -> x8, local copies, waits for them, and re-layouts: 9.48 us -> 7.77 us
  transfers between devices with their start and end apart: 5 -> 5, of which waited for: 4 -> 4; matrix products, arithmetic and copies ran while one was open for 6% -> 8% of each run, Pallas kernels for 0% -> 0%
where the time goes in v1:
time: 334 us; the launch traced here: 333 us
  waiting for transfers between devices  190 us (57%)
  blocking collectives  62.7 us (19%)
  starting transfers between devices  22.8 us (7%)
  matrix products  21.8 us (7%)
  local copies, waits for them, and re-layouts  21.1 us (6%)
  between operations  14.1 us (4%)
    ppermute x1, waiting for transfers between devices, partner(): lax.ppermute(shard, axis, [(i, i ^ 1 << apart) for i in range(lax.axis_si...  92.1 us
    psum x1, blocking collectives, local(): value_cot16 = lax.psum(value_terms, 'ctx').astype(jnp.bfloat16)  62.7 us
    all_gather x1, waiting for transfers between devices, local(): lax.all_gather(own_weight, 'ctx', axis=0, tiled=True)  44.6 us
    all_to_all x1, waiting for transfers between devices, local(): lax.all_to_all(jnp.stack([key_states[0]] * lax.axis_size('ctx')), 'ctx',...  33.3 us
    all_gather x1, waiting for transfers between devices, local(): lax.all_gather(local_values, 'ctx', axis=0, tiled=True)  19.1 us
    all_to_all x1, starting transfers between devices, local(): lax.all_to_all(jnp.stack([key_states[0]] * lax.axis_size('ctx')), 'ctx',...  10.3 us
    dot_general x1, matrix products, local(): jnp.einsum('kgij,ikgd->jkd', probabilities, cot_heads, preferred_element_...  8.46 us
    unnamed x8, local copies, waits for them, and re-layouts  7.77 us
  transfers between devices with their start and end apart: 5, of which 4 were waited for; matrix products, arithmetic and copies ran while one was open for 8% of the time, Pallas kernels for 0%

profile of v1, /device:TPU:1, one launch (start us, length us, event | category | flops | bytes accessed | tf_op | source)
XLA Modules:
  0.0 333.2 jit_solution(6353384324297421988)
XLA Ops:
  7.2 0.0 copy-start
  7.2 0.0 all-gather.6.cloned.1.call-start
  7.2 0.7 all-gather.6.cloned.1.call-update
  7.9 1.0 copy.43
  8.9 1.1 stack.12
  10.1 10.3 %all-to-all-start = ((bf16[8,128,512]{1,2,0:T(8,128)(2,1)}), bf16[8,128,512]{1,2,0:T(8,128)(2,1)S(1)}, u32[]{:S(2)}, u32[]{:S(2)}) async-start(bf16[8,128,512]{1,2,0:T(8,128)(2,1)} %stack.12), calls=%async_computation | async-start | bytes 2097152 | tf_op jit(solution)/shard_map/all_to_all | solution.py:38
  20.4 2.2 copy.51
  22.6 33.3 %all-to-all-done = bf16[8,128,512]{1,2,0:T(8,128)(2,1)S(1)} async-done(((bf16[8,128,512]{1,2,0:T(8,128)(2,1)}), bf16[8,128,512]{1,2,0:T(8,128)(2,1)S(1)}, u32[]{:S(2)}, u32[]{:S(2)}) %all-to-all-start) | async-done | bytes 1048608 | tf_op jit(solution)/shard_map/all_to_all | solution.py:38
  55.9 6.5 %all-to-all-start.1 = ((bf16[128,8,512]{0,2,1:T(8,128)(2,1)}), bf16[128,8,512]{0,2,1:T(8,128)(2,1)S(1)}, u32[]{:S(2)}, u32[]{:S(2)}) async-start(bf16[128,8,512]{0,2,1:T(8,128)(2,1)} %bitcast.16), calls=%async_computation.1 | async-start | bytes 2097152 | tf_op jit(solution)/shard_map/all_to_all | solution.py:27
  62.4 0.0 all-gather.4.cloned.1.call-start
  62.4 44.6 %all-gather.6.cloned.1.call-done = bf16[1,4096,512]{2,1,0:T(8,128)(2,1)} async-done(((bf16[1,512,512]{2,1,0:T(8,128)(2,1)}), bf16[1,4096,512]{2,1,0:T(8,128)(2,1)}) %all-gather.6.cloned.1.call-update) | async-done | bytes 4194320 | tf_op jit(solution)/shard_map/all_gather | solution.py:31
  106.9 3.9 %fusion.19 = bf16[128,512]{1,0:T(8,128)(2,1)} fusion(bf16[1,4096,512]{2,1,0:T(8,128)(2,1)} %all-gather.6.cloned.1.call-done, bf16[1,128,4096]{2,1,0:T(8,128)(2,1)} %param.7), kind=kOutput, calls=%fused_computation.22 | convolution fusion | flops 537001984 | bytes 5373952 | tf_op jit(solution)/shard_map/dot_general | solution.py:29
  110.8 0.0 all-gather.4.cloned.1.call-update
  110.9 0.0 copy-done
  110.9 0.2 copy.41
  111.1 2.2 reshape_squeeze.3
  113.3 2.2 copy.49
  115.5 1.3 copy.42
  116.8 2.0 copy.53
  118.8 0.1 iota_compare_fusion
  118.9 1.7 copy.44
  120.6 1.5 reshape_reshape.3
  122.1 0.0 all-to-all-done.1
  122.1 1.3 copy.52
  123.4 7.0 %fusion.48 = (f32[4,4,128]{2,1,0:T(4,128)S(1)}, f32[4,4,128,1024]{2,3,1,0:T(8,128)}) fusion(pred[128,1024]{0,1:T(8,128)(4,1)S(1)} %iota_compare_fusion, bf16[1024,4,128]{0,2,1:T(8,128)(2,1)S(1)} %reshape_reshape.3, bf16[128,4,4,128]{3,2,1,0:T(4,128)(2,1)} %reshape_squeeze.3), kind=kOutput, calls=%fused_computation.48 | convolution fusion | flops 545260544 | bytes 10100736 | tf_op jit(solution)/shard_map/sub | solution.py:54
  130.4 19.1 %all-gather.4.cloned.1.call-done = bf16[1024,512]{1,0:T(8,128)(2,1)} async-done(((bf16[128,512]{1,0:T(8,128)(2,1)}), bf16[1024,512]{1,0:T(8,128)(2,1)}) %all-gather.4.cloned.1.call-update) | async-done | bytes 1048592 | tf_op jit(solution)/shard_map/all_gather | solution.py:40
  149.5 2.3 copy.61
  151.7 8.5 %fusion.15 = f32[4,128,1024,1]{2,1,3,0:T(8,128)S(1)} fusion(f32[128,4,4,128]{0,3,2,1:T(8,128)} %bitcast.113, bf16[1024,4,128,1]{0,2,3,1:T(8,128)(2,1)} %bitcast.115, f32[4,4,128,1024]{2,3,1,0:T(8,128)} %get-tuple-element.13, f32[4,4,128]{2,1,0:T(4,128)S(1)} %get-tuple-element.12), kind=kOutput, calls=%fused_computation.20 | convolution fusion | flops 1082916864 | bytes 12591104 | tf_op jit(solution)/shard_map/kgij,ikgd->jkd/dot_general | solution.py:62
  160.2 62.7 %all-reduce.1 = bf16[1024,512]{0,1:T(8,128)(2,1)} all-reduce(f32[1024,512]{0,1:T(8,128)S(1)} %bitcast.112), channel_id=1, replica_groups=mesh['rep'=64,'ctx'=8] {'ctx'}, use_global_device_ids=true, to_apply=%region_2.3 | all-reduce | flops 524288 | bytes 3145728 | tf_op jit(solution)/shard_map/psum | solution.py:66
  222.9 2.5 fusion.13
  225.4 0.2 fusion.37
  225.6 0.2 pad_maximum_fusion
  225.8 6.0 %collective-permute-start = (f32[2,512,512]{1,2,0:T(8,128)S(1)}, f32[2,512,512]{1,2,0:T(8,128)S(1)}, u32[]{:S(2)}, u32[]{:S(2)}) collective-permute-start(f32[2,512,512]{1,2,0:T(8,128)S(1)} %pad_maximum_fusion), channel_id=1, source_target_pairs={{0,64},{8,72},{16,80},{24,88},{32,96},{40,104},{48,112},{56,120},{... | collective-permute-start | bytes 6291464 | tf_op jit(solution)/shard_map/ppermute | solution.py:15
  231.8 92.1 %collective-permute-done = f32[2,512,512]{1,2,0:T(8,128)S(1)} collective-permute-done((f32[2,512,512]{1,2,0:T(8,128)S(1)}, f32[2,512,512]{1,2,0:T(8,128)S(1)}, u32[]{:S(2)}, u32[]{:S(2)}) %collective-permute-start) | collective-permute-done | bytes 2097184 | tf_op jit(solution)/shard_map/ppermute | solution.py:15
  323.9 0.5 fusion.39
  324.4 1.0 copy.54
  325.4 1.0 copy.55
  (1 shorter events, 0.0 us)
Async XLA Ops:
  7.2 103.7 %copy-start = (bf16[1,512,512]{2,1,0:T(8,128)(2,1)S(1)}, bf16[1,512,512]{2,1,0:T(8,128)(2,1)}, u32[]{:S(2)}) copy-start(bf16[1,512,512]{2,1,0:T(8,128)(2,1)} %param.11) | copy-start | bytes 1572868
  7.2 99.8 %all-gather.6.cloned.1.call-start = ((), (), s32[]{:S(2)}) async-start(), calls=%async_computation.3 | async-start | bytes 4718592 | tf_op jit(solution)/shard_map/all_gather | solution.py:31
  10.1 45.8 %all-to-all-start = ((bf16[8,128,512]{1,2,0:T(8,128)(2,1)}), bf16[8,128,512]{1,2,0:T(8,128)(2,1)S(1)}, u32[]{:S(2)}, u32[]{:S(2)}) async-start(bf16[8,128,512]{1,2,0:T(8,128)(2,1)} %stack.12), calls=%async_computation | async-start | bytes 2097152 | tf_op jit(solution)/shard_map/all_to_all | solution.py:38
  55.9 66.2 %all-to-all-start.1 = ((bf16[128,8,512]{0,2,1:T(8,128)(2,1)}), bf16[128,8,512]{0,2,1:T(8,128)(2,1)S(1)}, u32[]{:S(2)}, u32[]{:S(2)}) async-start(bf16[128,8,512]{0,2,1:T(8,128)(2,1)} %bitcast.16), calls=%async_computation.1 | async-start | bytes 2097152 | tf_op jit(solution)/shard_map/all_to_all | solution.py:27
  62.4 87.1 %all-gather.4.cloned.1.call-start = ((), (), s32[]{:S(2)}) async-start(), calls=%async_computation.2 | async-start | bytes 1179648 | tf_op jit(solution)/shard_map/all_gather | solution.py:40
  225.8 98.1 %collective-permute-start = (f32[2,512,512]{1,2,0:T(8,128)S(1)}, f32[2,512,512]{1,2,0:T(8,128)S(1)}, u32[]{:S(2)}, u32[]{:S(2)}) collective-permute-start(f32[2,512,512]{1,2,0:T(8,128)S(1)} %pad_maximum_fusion), channel_id=1, source_target_pairs={{0,64},{8,72},{16,80},{24,88},{32,96},{40,104},{48,112},{56,120},{... | collective-permute-start | bytes 6291464 | tf_op jit(solution)/shard_map/ppermute | solution.py:15
Sparse Core Ops, SparseCore 0:
  10.1 96.8 all-gather.5
  111.0 38.4 all-gather.3
